TPU v7x, 256 devices: a whole 4x4x8 slice. The times are simulated.
256 devices in a mesh: lon: 16 (over z, y_lo), lat: 8 (over x, y_hi), lev: 2 (over core).
Axes of the slice: x: 4, y: 4 (y_hi: 2, y_lo: 2; y = y_hi * 2 + y_lo), z: 8, core: 2. Of those that a mesh axis runs over, the one named last changes fastest.
Arguments:
- adjoint_in: float32 [9, 16, 128, 2048], P(None, 'lev', 'lat', 'lon'), may hold values from -6 to 6
- trajectory: bfloat16 [3, 9, 16, 128, 2048], P(None, None, 'lev', 'lat', 'lon'), may hold values from 0.5 to 2
- courant: float32 [2, 16, 128, 2048], P(None, 'lev', 'lat', 'lon'), may hold values from -0.4 to 0.4
- mixing: float32 [16, 128, 2048], P('lev', 'lat', 'lon'), may hold values from 0.02 to 0.2
- coag_rates: float32 [6, 16], replicated, may hold values from 0.02 to 0.2
- settle_speed: float32 [8, 9], replicated, may hold values from 0.01 to 0.2
- settle_class: int32 [16], replicated, may hold values from 0 to 7
- emis_profile: float32 [16], replicated, may hold values from 0.1 to 1
- emis_coef: float32 [9], replicated, may hold values from 0.5 to 2
- land_mask: int32 [128, 2048], P('lat', 'lon'), may hold values 0 or 1
- source_mask: int32 [128, 2048], P('lat', 'lon'), may hold values 0 or 1
Outputs:
- adjoint_out: float32 [9, 16, 128, 2048], P(None, 'lev', 'lat', 'lon')
- emis_grad: float32 [3, 128, 2048], P(None, 'lat', 'lon')
All inputs are finite; a program needn't handle non-finite values. No bound on the sum of `land_mask` or of `source_mask` on one device may be relied on, other than what follows from the above.
Results may differ from a plain program's by a relative error of at most 0.0003.
Values may be sent and summed in bfloat16 or wider, within the bound.
A program may use at most 64 MiB of HBM per device.

v0:
```python
import jax
import jax.numpy as jnp
from jax import lax
from jax.sharding import PartitionSpec as P


def with_halo(cells, sides, width, closed):
    for axis, dim in sides:
        count = lax.axis_size(axis)
        ends = count if closed else count - 1
        head = lax.slice_in_dim(cells, 0, width, axis=dim)
        tail = lax.slice_in_dim(cells, cells.shape[dim] - width, cells.shape[dim], axis=dim)
        cells = jnp.concatenate(
            [
                lax.ppermute(tail, axis, [(i, (i + 1) % count) for i in range(ends)]),
                cells,
                lax.ppermute(head, axis, [((i + 1) % count, i) for i in range(ends)]),
            ],
            axis=dim,
        )
    return cells


def slab(field, axis, start, length):
    return lax.slice_in_dim(field, start, start + length, axis=axis)


def transport(padded, courant_pad, axis, length):
    courant_wide = courant_pad[None]
    diff_face = slab(padded, axis, 0, length + 3) - slab(padded, axis, 1, length + 3)
    face_speed = slab(courant_wide, axis, 0, length + 3)
    forward_part = jnp.maximum(face_speed, 0.0) * diff_face
    backward_part = jnp.minimum(face_speed, 0.0) * diff_face
    return (
        -1.5 * slab(forward_part, axis, 2, length)
        + 0.5 * slab(forward_part, axis, 3, length)
        - 1.5 * slab(backward_part, axis, 1, length)
        + 0.5 * slab(backward_part, axis, 0, length)
    )


def vertical(padded, mixing_pad, speeds, deposit):
    depth_count = padded.shape[1] - 2
    mixing_below = mixing_pad[:depth_count]
    mixing_above = mixing_pad[1 : depth_count + 1]
    speed_level = speeds[:, :, None, None]
    centre = padded[:, 1 : depth_count + 1]
    return (
        centre * (1.0 - mixing_above - mixing_below - speed_level - deposit)
        + padded[:, :depth_count] * (mixing_below + speed_level)
        + padded[:, 2:] * mixing_above
    )


def coag_increment(state, rates):
    rate_grid = rates[:, :, None, None]
    number = [state[0], state[3], state[6]]
    volume = [state[1], state[4], state[7]]
    moment_six = [state[2], state[5], state[8]]
    pair_rate = {(0, 1): rate_grid[3], (0, 2): rate_grid[4], (1, 2): rate_grid[5]}
    outputs = []
    for mode_index in range(3):
        d_number = -rate_grid[mode_index] * number[mode_index] * number[mode_index]
        d_volume = jnp.zeros_like(number[mode_index])
        d_moment = rate_grid[mode_index] * volume[mode_index] * volume[mode_index]
        for other_mode in range(3):
            if other_mode > mode_index:
                pair = pair_rate[mode_index, other_mode]
                d_number = d_number - pair * number[mode_index] * number[other_mode]
                d_volume = d_volume - pair * volume[mode_index] * number[other_mode]
                d_moment = d_moment - pair * moment_six[mode_index] * number[other_mode]
            if other_mode < mode_index:
                pair = pair_rate[other_mode, mode_index]
                d_volume = d_volume + pair * volume[other_mode] * number[mode_index]
                d_moment = d_moment + pair * (
                    moment_six[other_mode] * number[mode_index]
                    + 2.0 * volume[other_mode] * volume[mode_index]
                )
        outputs.extend([d_number, d_volume, d_moment])
    return jnp.stack(outputs)


def coag_adjoint(adjoint, state, rates):
    primal_out, pullback = jax.vjp(lambda value: coag_increment(value, rates), state)
    return adjoint + pullback(adjoint)[0]


def emission_part(adjoint, profile, emis_coef, source):
    weighted = adjoint * (emis_coef[:, None, None, None] * profile[None, :, None, None])
    per_tracer = jnp.sum(weighted, axis=1)
    per_mode = jnp.sum(per_tracer.reshape(3, 3, per_tracer.shape[1], per_tracer.shape[2]), axis=1)
    return per_mode * source


def sides(field, lat_index, row_count, lat_count):
    lon_pad = with_halo(field, (("lon", 3),), 2, True)
    lat_pad = with_halo(field, (("lat", 2),), 2, False)
    return (lon_pad, lat_pad)


def planes(field):
    return with_halo(field, (("lev", 1),), 1, False)


def run_split(
    adjoint_in,
    trajectory,
    winds,
    mixing_top,
    coag_rates,
    speeds_all,
    emis_profile,
    emis_coef,
    dep_rows,
    source,
):
    depth_count = adjoint_in.shape[1]
    row_count = adjoint_in.shape[2]
    col_count = adjoint_in.shape[3]
    lev_index = lax.axis_index("lev")
    lat_index = lax.axis_index("lat")
    lat_count = lax.axis_size("lat")
    level_global = lev_index * depth_count + jnp.arange(depth_count, dtype=jnp.int32)
    level_start = lev_index * depth_count
    rates_own = lax.dynamic_slice_in_dim(coag_rates, level_start, depth_count, 1)
    profile_own = lax.dynamic_slice_in_dim(emis_profile, level_start, depth_count, 0)
    wind_lon, wind_lat = sides(winds, lat_index, row_count, lat_count)
    east_pad = wind_lon[0]
    north_pad = wind_lat[1]
    mixing_pad = planes(mixing_top[None])[0]
    speeds_used = lax.dynamic_slice_in_dim(speeds_all, level_start, depth_count, 1)
    surface = (level_global == 0).astype(jnp.float32)
    deposit = dep_rows[None] * surface[:, None, None]
    adjoint = adjoint_in
    emis_grad = jnp.zeros((3, row_count, col_count), jnp.float32)
    for step_index in range(trajectory.shape[0] - 1, -1, -1):
        emis_grad = emis_grad + emission_part(adjoint, profile_own, emis_coef, source)
        adjoint = coag_adjoint(adjoint, trajectory[step_index].astype(jnp.float32), rates_own)
        adjoint = vertical(planes(adjoint), mixing_pad, speeds_used, deposit)
        lon_pad, lat_pad = sides(adjoint, lat_index, row_count, lat_count)
        adjoint = (
            adjoint
            + transport(lon_pad, east_pad, 3, col_count)
            + transport(lat_pad, north_pad, 2, row_count)
        )
    emis_grad = lax.psum(emis_grad, "lev")
    return (adjoint, emis_grad)


def shards(
    adjoint_in,
    trajectory,
    courant,
    mixing,
    coag_rates,
    settle_speed,
    settle_class,
    emis_profile,
    emis_coef,
    land_mask,
    source_mask,
):
    depth_count = adjoint_in.shape[1]
    row_count = adjoint_in.shape[2]
    lev_index = lax.axis_index("lev")
    lat_index = lax.axis_index("lat")
    lat_count = lax.axis_size("lat")
    level_total = settle_class.shape[0]
    row_global = lat_index * row_count + jnp.arange(row_count, dtype=jnp.int32)
    top_row = (row_global == row_count * lat_count - 1)[None, :, None]
    winds = jnp.stack([courant[0], jnp.where(top_row, 0.0, courant[1])])
    level_global = lev_index * depth_count + jnp.arange(depth_count, dtype=jnp.int32)
    mixing_top = jnp.where((level_global == level_total - 1)[:, None, None], 0.0, mixing)
    choose = (
        settle_class[:, None] == jnp.arange(settle_speed.shape[0], dtype=jnp.int32)[None, :]
    ).astype(jnp.float32)
    speeds_all = jnp.dot(choose, settle_speed, precision=lax.Precision.HIGHEST).T
    dep_rows = 0.1 + 0.3 * land_mask.astype(jnp.float32)
    source = source_mask.astype(jnp.float32)
    return run_split(
        adjoint_in,
        trajectory,
        winds,
        mixing_top,
        coag_rates,
        speeds_all,
        emis_profile,
        emis_coef,
        dep_rows,
        source,
    )


def solution(mesh):
    return jax.shard_map(
        shards,
        mesh=mesh,
        in_specs=(
            P(None, "lev", "lat", "lon"),
            P(None, None, "lev", "lat", "lon"),
            P(None, "lev", "lat", "lon"),
            P("lev", "lat", "lon"),
            P(),
            P(),
            P(),
            P(),
            P(),
            P("lat", "lon"),
            P("lat", "lon"),
        ),
        out_specs=(P(None, "lev", "lat", "lon"), P(None, "lat", "lon")),
        check_vma=False,
    )
```

profile of v0, /device:TPU:6, one launch (start us, length us, event | category | flops | bytes accessed | tf_op | source)
XLA Modules:
  0.0 130.4 jit_solution(11100671563132194854)
XLA Ops:
  0.7 0.8 constant_dynamic-slice_fusion
  1.5 1.4 %slice_convert_fusion = (f32[1,9,8,16,128]{4,3,2,1,0:T(8,128)S(1)}, f32[1,9,8,16,128]{4,3,2,1,0:T(8,128)S(1)}, f32[1,9,8,16,128]{4,3,2,1,0:T(8,128)S(1)}) fusion(bf16[3,9,8,16,128]{4,3,2,1,0:T(8,128)(2,1)} %param.12), kind=kLoop, calls=%fused_computation.97 | loop fusion | flops 442368 | bytes 2654208 | tf_op jit(solution)/shard_map/convert_element_type | solution.py:138
  3.8 0.7 fusion.59
  4.4 1.7 %collective-permute-start.1 = (f32[9,1,16,128]{3,2,1,0:T(8,128)}, f32[9,1,16,128]{3,2,1,0:T(8,128)S(1)}, u32[]{:S(2)}, u32[]{:S(2)}) collective-permute-start(f32[9,1,16,128]{3,2,1,0:T(8,128)} %get-tuple-element.54), channel_id=1, source_target_pairs={{0,1},{2,3},{4,5},{6,7},{8,9},{10,11},{12,13},{14,15},{16,17},{18,... | collective-permute-start | bytes 221192 | tf_op jit(solution)/shard_map/ppermute | solution.py:15
  6.2 1.3 collective-permute-start.2
  7.6 3.0 %collective-permute-start = (f32[1,1,16,128]{3,2,1,0:T(8,128)S(1)}, f32[1,1,16,128]{3,2,1,0:T(8,128)S(1)}, u32[]{:S(2)}, u32[]{:S(2)}) collective-permute-start(f32[1,1,16,128]{3,2,1,0:T(8,128)S(1)} %slice.569), channel_id=1, source_target_pairs={{0,1},{2,3},{4,5},{6,7},{8,9},{10,11},{12,13},{14,15},{16,17},{18,... | collective-permute-start | bytes 24584 | tf_op jit(solution)/shard_map/ppermute | solution.py:15
  10.8 1.7 %collective-permute-start.3 = (f32[2,8,16,2]{3,2,1,0:T(8,128)S(1)}, f32[2,8,16,2]{3,2,1,0:T(8,128)S(1)}, u32[]{:S(2)}, u32[]{:S(2)}) collective-permute-start(f32[2,8,16,2]{3,2,1,0:T(8,128)S(1)} %get-tuple-element.60), channel_id=1, source_target_pairs={{0,16},{16,32},{32,48},{48,64},{64,80},{80,96},{96,112},{112,128},... | collective-permute-start | bytes 6152 | tf_op jit(solution)/shard_map/ppermute | solution.py:15
  12.5 5.4 %collective-permute-start.4 = (f32[2,8,16,2]{3,2,1,0:T(8,128)S(1)}, f32[2,8,16,2]{3,2,1,0:T(8,128)S(1)}, u32[]{:S(2)}, u32[]{:S(2)}) collective-permute-start(f32[2,8,16,2]{3,2,1,0:T(8,128)S(1)} %get-tuple-element.61), channel_id=1, source_target_pairs={{16,0},{32,16},{48,32},{64,48},{80,64},{96,80},{112,96},{128,112},... | collective-permute-start | bytes 6152 | tf_op jit(solution)/shard_map/ppermute | solution.py:17
  18.4 0.7 dynamic_slice.11
  19.0 1.8 %collective-permute-done.3 = f32[2,8,16,2]{3,2,1,0:T(8,128)S(1)} collective-permute-done((f32[2,8,16,2]{3,2,1,0:T(8,128)S(1)}, f32[2,8,16,2]{3,2,1,0:T(8,128)S(1)}, u32[]{:S(2)}, u32[]{:S(2)}) %collective-permute-start.3) | collective-permute-done | bytes 2080 | tf_op jit(solution)/shard_map/ppermute | solution.py:15
  20.8 4.9 %collective-permute-start.7 = (f32[2,8,2,128]{3,2,1,0:T(2,128)S(1)}, f32[2,8,2,128]{3,2,1,0:T(2,128)S(1)}, u32[]{:S(2)}, u32[]{:S(2)}) collective-permute-start(f32[2,8,2,128]{3,2,1,0:T(2,128)S(1)} %get-tuple-element.62), channel_id=1, source_target_pairs={{0,2},{2,4},{4,6},{6,8},{8,10},{10,12},{12,14},{1,3},{3,5},{5,7},{... | collective-permute-start | bytes 49160 | tf_op jit(solution)/shard_map/ppermute | solution.py:15
  25.8 3.3 %collective-permute-start.8 = (f32[2,8,2,128]{3,2,1,0:T(2,128)S(1)}, f32[2,8,2,128]{3,2,1,0:T(2,128)S(1)}, u32[]{:S(2)}, u32[]{:S(2)}) collective-permute-start(f32[2,8,2,128]{3,2,1,0:T(2,128)S(1)} %get-tuple-element.63), channel_id=1, source_target_pairs={{2,0},{4,2},{6,4},{8,6},{10,8},{12,10},{14,12},{3,1},{5,3},{7,5},{... | collective-permute-start | bytes 49160 | tf_op jit(solution)/shard_map/ppermute | solution.py:17
  29.2 0.7 fusion.35
  30.0 2.9 %collective-permute-done.8 = f32[2,8,2,128]{3,2,1,0:T(2,128)S(1)} collective-permute-done((f32[2,8,2,128]{3,2,1,0:T(2,128)S(1)}, f32[2,8,2,128]{3,2,1,0:T(2,128)S(1)}, u32[]{:S(2)}, u32[]{:S(2)}) %collective-permute-start.8) | collective-permute-done | bytes 16416 | tf_op jit(solution)/shard_map/ppermute | solution.py:17
  32.9 0.7 maximum_bitcast_fusion.1
  33.7 0.6 copy-done.16
  34.3 1.1 fusion.1
  35.5 1.2 fusion.57
  36.6 2.2 %copy.101 = f32[9,8,16,2]{2,1,3,0:T(8,128)} copy(f32[9,8,16,2]{3,2,1,0:T(8,128)} %get-tuple-element.50) | data formatting | bytes 18432 | tf_op jit(solution)/shard_map/slice | solution.py:12
  38.8 2.2 %copy.102 = f32[9,8,16,2]{2,1,3,0:T(8,128)} copy(f32[9,8,16,2]{3,2,1,0:T(8,128)} %get-tuple-element.51) | data formatting | bytes 18432 | tf_op jit(solution)/shard_map/slice | solution.py:11
  41.0 4.1 %collective-permute-start.6 = (f32[9,8,16,2]{2,1,3,0:T(8,128)}, f32[9,8,16,2]{2,1,3,0:T(8,128)}, u32[]{:S(2)}, u32[]{:S(2)}) collective-permute-start(f32[9,8,16,2]{2,1,3,0:T(8,128)} %copy.102), channel_id=1, source_target_pairs={{16,0},{32,16},{48,32},{64,48},{80,64},{96,80},{112,96},{128,112},... | collective-permute-start | bytes 27656 | tf_op jit(solution)/shard_map/ppermute | solution.py:17
  45.2 0.6 copy.105
  45.8 2.0 %collective-permute-start.9 = (f32[9,8,2,128]{3,1,2,0:T(8,128)}, f32[9,8,2,128]{3,1,2,0:T(8,128)}, u32[]{:S(2)}, u32[]{:S(2)}) collective-permute-start(f32[9,8,2,128]{3,1,2,0:T(8,128)} %copy.105), channel_id=1, source_target_pairs={{0,2},{2,4},{4,6},{6,8},{8,10},{10,12},{12,14},{1,3},{3,5},{5,7},{... | collective-permute-start | bytes 221192 | tf_op jit(solution)/shard_map/ppermute | solution.py:15
  47.9 0.6 copy.106
  48.5 6.2 %collective-permute-start.10 = (f32[9,8,2,128]{3,1,2,0:T(8,128)}, f32[9,8,2,128]{3,1,2,0:T(8,128)}, u32[]{:S(2)}, u32[]{:S(2)}) collective-permute-start(f32[9,8,2,128]{3,1,2,0:T(8,128)} %copy.106), channel_id=1, source_target_pairs={{2,0},{4,2},{6,4},{8,6},{10,8},{12,10},{14,12},{3,1},{5,3},{7,5},{... | collective-permute-start | bytes 221192 | tf_op jit(solution)/shard_map/ppermute | solution.py:17
  54.7 2.2 %copy.103 = f32[9,8,16,2]{3,2,1,0:T(8,128)} copy(f32[9,8,16,2]{2,1,3,0:T(8,128)} %collective-permute-done.5) | data formatting | bytes 18432 | tf_op jit(solution)/shard_map/ppermute | solution.py:15
  56.9 2.2 %copy.104 = f32[9,8,16,2]{3,2,1,0:T(8,128)} copy(f32[9,8,16,2]{2,1,3,0:T(8,128)} %collective-permute-done.6) | data formatting | bytes 18432 | tf_op jit(solution)/shard_map/ppermute | solution.py:17
  59.1 1.8 %pad_maximum_fusion = f32[9,8,16,132]{3,2,1,0:T(8,128)S(1)} fusion(f32[9,8,16,2]{3,2,1,0:T(8,128)} %copy.104, f32[9,8,16,128]{3,2,1,0:T(8,128)S(1)} %fusion.1, f32[9,8,16,2]{3,2,1,0:T(8,128)} %copy.103), kind=kLoop, calls=%fused_computation.3 | loop fusion | flops 304128 | bytes 1216512 | tf_op jit(solution)/shard_map/concatenate | solution.py:13
  61.4 1.0 copy.107
  62.4 0.9 copy.108
  63.7 0.7 copy-done.17
  64.4 0.7 fusion.25
  66.3 1.3 collective-permute-start.11
  67.6 1.3 collective-permute-start.12
  69.0 1.7 %collective-permute-done.12 = f32[9,1,16,128]{3,2,1,0:T(8,128)S(1)} collective-permute-done((f32[9,1,16,128]{3,2,1,0:T(8,128)S(1)}, f32[9,1,16,128]{3,2,1,0:T(8,128)S(1)}, u32[]{:S(2)}, u32[]{:S(2)}) %collective-permute-start.12) | collective-permute-done | bytes 73760 | tf_op jit(solution)/shard_map/ppermute | solution.py:17
  71.0 1.2 fusion.54
  72.2 2.2 %copy.109 = f32[9,8,16,2]{2,1,3,0:T(8,128)} copy(f32[9,8,16,2]{3,2,1,0:T(8,128)} %get-tuple-element.44) | data formatting | bytes 18432 | tf_op jit(solution)/shard_map/slice | solution.py:12
  74.4 2.2 %copy.110 = f32[9,8,16,2]{2,1,3,0:T(8,128)} copy(f32[9,8,16,2]{3,2,1,0:T(8,128)} %get-tuple-element.45) | data formatting | bytes 18432 | tf_op jit(solution)/shard_map/slice | solution.py:11
  76.6 4.1 %collective-permute-start.14 = (f32[9,8,16,2]{2,1,3,0:T(8,128)}, f32[9,8,16,2]{2,1,3,0:T(8,128)}, u32[]{:S(2)}, u32[]{:S(2)}) collective-permute-start(f32[9,8,16,2]{2,1,3,0:T(8,128)} %copy.110), channel_id=1, source_target_pairs={{16,0},{32,16},{48,32},{64,48},{80,64},{96,80},{112,96},{128,112},... | collective-permute-start | bytes 27656 | tf_op jit(solution)/shard_map/ppermute | solution.py:17
  80.8 0.6 copy.113
  81.4 1.9 %collective-permute-start.15 = (f32[9,8,2,128]{3,1,2,0:T(8,128)}, f32[9,8,2,128]{3,1,2,0:T(8,128)}, u32[]{:S(2)}, u32[]{:S(2)}) collective-permute-start(f32[9,8,2,128]{3,1,2,0:T(8,128)} %copy.113), channel_id=1, source_target_pairs={{0,2},{2,4},{4,6},{6,8},{8,10},{10,12},{12,14},{1,3},{3,5},{5,7},{... | collective-permute-start | bytes 221192 | tf_op jit(solution)/shard_map/ppermute | solution.py:15
  83.3 0.6 copy.114
  84.0 6.5 %collective-permute-start.16 = (f32[9,8,2,128]{3,1,2,0:T(8,128)}, f32[9,8,2,128]{3,1,2,0:T(8,128)}, u32[]{:S(2)}, u32[]{:S(2)}) collective-permute-start(f32[9,8,2,128]{3,1,2,0:T(8,128)} %copy.114), channel_id=1, source_target_pairs={{2,0},{4,2},{6,4},{8,6},{10,8},{12,10},{14,12},{3,1},{5,3},{7,5},{... | collective-permute-start | bytes 221192 | tf_op jit(solution)/shard_map/ppermute | solution.py:17
  90.5 2.2 %copy.111 = f32[9,8,16,2]{3,2,1,0:T(8,128)} copy(f32[9,8,16,2]{2,1,3,0:T(8,128)} %collective-permute-done.13) | data formatting | bytes 18432 | tf_op jit(solution)/shard_map/ppermute | solution.py:15
  92.7 2.2 %copy.112 = f32[9,8,16,2]{3,2,1,0:T(8,128)} copy(f32[9,8,16,2]{2,1,3,0:T(8,128)} %collective-permute-done.14) | data formatting | bytes 18432 | tf_op jit(solution)/shard_map/ppermute | solution.py:17
  94.9 1.8 %pad_maximum_fusion.1 = f32[9,8,16,132]{3,2,1,0:T(8,128)S(1)} fusion(f32[9,8,16,2]{3,2,1,0:T(8,128)} %copy.112, f32[9,8,16,128]{3,2,1,0:T(8,128)S(1)} %fusion.3, f32[9,8,16,2]{3,2,1,0:T(8,128)} %copy.111), kind=kLoop, calls=%fused_computation.4 | loop fusion | flops 304128 | bytes 1216512 | tf_op jit(solution)/shard_map/concatenate | solution.py:13
  96.7 0.5 broadcast_multiply_fusion.4
  97.2 1.0 copy.115
  98.2 0.9 copy.116
  99.5 0.6 copy-done.10
  100.2 1.6 %multiply_reduce_fusion.1 = (f32[9,16,128]{2,1,0:T(8,128)}, f32[9,16,128]{2,1,0:T(8,128)}, f32[9,16,128]{2,1,0:T(8,128)}, f32[9,8,16,128]{3,2,1,0:T(8,128)S(1)}) fusion(f32[9,8,16,128]{3,2,1,0:T(8,128)S(1)} %fusion.25, f32[9,8]{1,0:T(8,128)S(1)} %broadcast_multiply_fusion.13, f32[9,8,16,128]{3,2,1,0:T(8,128)S(1)} %copy-done.1, ...), kind=kLoop, calls=%fused_computation.79 | loop fusion | flops 4663296 | bytes 7709248 | tf_op jit(solution)/shard_map/reduce_sum | solution.py:90
  103.2 1.3 collective-permute-start.17
  104.5 1.3 collective-permute-start.18
  105.8 5.0 %psum.7 = f32[3,16,128]{2,1,0:T(8,128)} all-reduce(f32[3,16,128]{2,1,0:T(8,128)S(1)} %add_multiply_fusion.3), channel_id=1, replica_groups=mesh['lon'=16,'lat'=8,'lev'=2] {'lev'}, use_global_device_ids=true, to_apply=%region_6.7 | all-reduce | flops 6144 | bytes 49152 | tf_op jit(solution)/shard_map/psum | solution.py:146
  111.2 0.5 copy.117
  111.8 0.5 copy.118
  112.3 4.2 %collective-permute-start.20 = (f32[9,8,16,2]{2,1,3,0:T(8,128)S(1)}, f32[9,8,16,2]{2,1,3,0:T(8,128)}, u32[]{:S(2)}, u32[]{:S(2)}) collective-permute-start(f32[9,8,16,2]{2,1,3,0:T(8,128)S(1)} %copy.118), channel_id=1, source_target_pairs={{16,0},{32,16},{48,32},{64,48},{80,64},{96,80},{112,96},{128,112},... | collective-permute-start | bytes 27656 | tf_op jit(solution)/shard_map/ppermute | solution.py:17
  116.5 1.9 %collective-permute-start.21 = (f32[9,8,2,128]{3,1,2,0:T(8,128)S(1)}, f32[9,8,2,128]{3,1,2,0:T(8,128)S(1)}, u32[]{:S(2)}, u32[]{:S(2)}) collective-permute-start(f32[9,8,2,128]{3,1,2,0:T(8,128)S(1)} %copy.121), channel_id=1, source_target_pairs={{0,2},{2,4},{4,6},{6,8},{8,10},{10,12},{12,14},{1,3},{3,5},{5,7},{... | collective-permute-start | bytes 221192 | tf_op jit(solution)/shard_map/ppermute | solution.py:15
  118.5 6.3 %collective-permute-start.22 = (f32[9,8,2,128]{3,1,2,0:T(8,128)S(1)}, f32[9,8,2,128]{3,1,2,0:T(8,128)S(1)}, u32[]{:S(2)}, u32[]{:S(2)}) collective-permute-start(f32[9,8,2,128]{3,1,2,0:T(8,128)S(1)} %copy.122), channel_id=1, source_target_pairs={{2,0},{4,2},{6,4},{8,6},{10,8},{12,10},{14,12},{3,1},{5,3},{7,5},{... | collective-permute-start | bytes 221192 | tf_op jit(solution)/shard_map/ppermute | solution.py:17
  124.8 0.5 copy.119
  125.3 1.4 %copy.120 = f32[9,8,16,2]{3,2,1,0:T(8,128)S(1)} copy(f32[9,8,16,2]{2,1,3,0:T(8,128)} %collective-permute-done.20) | data formatting | bytes 18432 | tf_op jit(solution)/shard_map/ppermute | solution.py:17
  126.7 0.5 pad_maximum_fusion.2
  127.9 0.6 copy-done.4
  128.8 1.6 %fusion.7 = f32[9,8,16,128]{3,2,1,0:T(8,128)} fusion(f32[9,8,19,128]{3,2,1,0:T(8,128)S(1)} %get-tuple-element.30, f32[9,8,19,128]{3,2,1,0:T(8,128)S(1)} %get-tuple-element.29, f32[9,8,16,131]{3,2,1,0:T(8,128)S(1)} %get-tuple-element.24, f32[9,8,16,131]{3,2,1,0:T(8,128)S(1)} %get-tuple-element.23, f32[8,16,128]{2,1,0:T(8,128)S(1)} %broadcast_select_fusion, ...), kind=kLoop, calls=%fused_computation.23 | loop fusion | flops 3833856 | bytes 6308128 | tf_op jit(solution)/shard_map/add | solution.py:142
  (154 shorter events, 7.3 us)
Async XLA Ops:
  0.6 17.4 %copy-start = (f32[8,9]{1,0:T(8,128)S(1)}, f32[8,9]{1,0:T(8,128)}, u32[]{:S(2)}) copy-start(f32[8,9]{1,0:T(8,128)} %param.16) | copy-start | bytes 868
  1.4 1.5 %copy-start.29 = (f32[8]{0:T(128)}, f32[8]{0:T(128)S(1)}, u32[]{:S(2)}) copy-start(f32[8]{0:T(128)S(1)} %get-tuple-element.70) | copy-start | bytes 100
  1.4 1.7 %copy-start.27 = (f32[8]{0:T(128)}, f32[8]{0:T(128)S(1)}, u32[]{:S(2)}) copy-start(f32[8]{0:T(128)S(1)} %get-tuple-element.69) | copy-start | bytes 100
  1.4 1.6 %copy-start.25 = (f32[8]{0:T(128)}, f32[8]{0:T(128)S(1)}, u32[]{:S(2)}) copy-start(f32[8]{0:T(128)S(1)} %get-tuple-element.76) | copy-start | bytes 100
  1.4 2.0 %copy-start.23 = (f32[8]{0:T(128)}, f32[8]{0:T(128)S(1)}, u32[]{:S(2)}) copy-start(f32[8]{0:T(128)S(1)} %get-tuple-element.75) | copy-start | bytes 100
  1.5 1.4 %copy-start.1 = (f32[9,8,16,128]{3,2,1,0:T(8,128)S(1)}, f32[9,8,16,128]{3,2,1,0:T(8,128)}, u32[]{:S(2)}) copy-start(f32[9,8,16,128]{3,2,1,0:T(8,128)} %param.11) | copy-start | bytes 1769476
  3.6 3.9 %copy-start.8 = (f32[8,16,128]{2,1,0:T(8,128)S(1)}, f32[8,16,128]{2,1,0:T(8,128)}, u32[]{:S(2)}) copy-start(f32[8,16,128]{2,1,0:T(8,128)} %param.14) | copy-start | bytes 196612
  3.6 7.0 %copy-start.20 = (f32[2,8,16,128]{3,2,1,0:T(8,128)S(1)}, f32[2,8,16,128]{3,2,1,0:T(8,128)}, u32[]{:S(2)}) copy-start(f32[2,8,16,128]{3,2,1,0:T(8,128)} %param.13) | copy-start | bytes 393220
  3.6 14.3 %copy-start.21 = (s32[16,128]{1,0:T(8,128)S(1)}, s32[16,128]{1,0:T(8,128)}, u32[]{:S(2)}) copy-start(s32[16,128]{1,0:T(8,128)} %param.20) | copy-start | bytes 24580
  3.6 14.4 %copy-start.34 = (s32[16]{0:T(128)S(1)}, s32[16]{0:T(128)}, u32[]{:S(2)}) copy-start(s32[16]{0:T(128)} %param.17) | copy-start | bytes 196
  3.7 14.6 %copy-start.35 = (f32[16]{0:T(128)S(1)}, f32[16]{0:T(128)}, u32[]{:S(2)}) copy-start(f32[16]{0:T(128)} %param.18) | copy-start | bytes 196
  4.4 29.2 %collective-permute-start.1 = (f32[9,1,16,128]{3,2,1,0:T(8,128)}, f32[9,1,16,128]{3,2,1,0:T(8,128)S(1)}, u32[]{:S(2)}, u32[]{:S(2)}) collective-permute-start(f32[9,1,16,128]{3,2,1,0:T(8,128)} %get-tuple-element.54), channel_id=1, source_target_pairs={{0,1},{2,3},{4,5},{6,7},{8,9},{10,11},{12,13},{14,15},{16,17},{18,... | collective-permute-start | bytes 221192 | tf_op jit(solution)/shard_map/ppermute | solution.py:15
  6.2 27.5 %collective-permute-start.2 = (f32[9,1,16,128]{3,2,1,0:T(8,128)}, f32[9,1,16,128]{3,2,1,0:T(8,128)S(1)}, u32[]{:S(2)}, u32[]{:S(2)}) collective-permute-start(f32[9,1,16,128]{3,2,1,0:T(8,128)} %get-tuple-element.55), channel_id=1, source_target_pairs={{1,0},{3,2},{5,4},{7,6},{9,8},{11,10},{13,12},{15,14},{17,16},{19,... | collective-permute-start | bytes 221192 | tf_op jit(solution)/shard_map/ppermute | solution.py:17
  7.5 10.5 %copy-start.31 = (pred[8]{0:T(512)(128)(4,1)}, pred[8]{0:T(512)(128)(4,1)S(1)}, u32[]{:S(2)}) copy-start(pred[8]{0:T(512)(128)(4,1)S(1)} %fusion.46) | copy-start | bytes 28
  7.6 21.7 %collective-permute-start = (f32[1,1,16,128]{3,2,1,0:T(8,128)S(1)}, f32[1,1,16,128]{3,2,1,0:T(8,128)S(1)}, u32[]{:S(2)}, u32[]{:S(2)}) collective-permute-start(f32[1,1,16,128]{3,2,1,0:T(8,128)S(1)} %slice.569), channel_id=1, source_target_pairs={{0,1},{2,3},{4,5},{6,7},{8,9},{10,11},{12,13},{14,15},{16,17},{18,... | collective-permute-start | bytes 24584 | tf_op jit(solution)/shard_map/ppermute | solution.py:15
  10.8 10.0 %collective-permute-start.3 = (f32[2,8,16,2]{3,2,1,0:T(8,128)S(1)}, f32[2,8,16,2]{3,2,1,0:T(8,128)S(1)}, u32[]{:S(2)}, u32[]{:S(2)}) collective-permute-start(f32[2,8,16,2]{3,2,1,0:T(8,128)S(1)} %get-tuple-element.60), channel_id=1, source_target_pairs={{0,16},{16,32},{32,48},{48,64},{64,80},{80,96},{96,112},{112,128},... | collective-permute-start | bytes 6152 | tf_op jit(solution)/shard_map/ppermute | solution.py:15
  12.5 13.3 %collective-permute-start.4 = (f32[2,8,16,2]{3,2,1,0:T(8,128)S(1)}, f32[2,8,16,2]{3,2,1,0:T(8,128)S(1)}, u32[]{:S(2)}, u32[]{:S(2)}) collective-permute-start(f32[2,8,16,2]{3,2,1,0:T(8,128)S(1)} %get-tuple-element.61), channel_id=1, source_target_pairs={{16,0},{32,16},{48,32},{64,48},{80,64},{96,80},{112,96},{128,112},... | collective-permute-start | bytes 6152 | tf_op jit(solution)/shard_map/ppermute | solution.py:17
  20.8 9.1 %collective-permute-start.7 = (f32[2,8,2,128]{3,2,1,0:T(2,128)S(1)}, f32[2,8,2,128]{3,2,1,0:T(2,128)S(1)}, u32[]{:S(2)}, u32[]{:S(2)}) collective-permute-start(f32[2,8,2,128]{3,2,1,0:T(2,128)S(1)} %get-tuple-element.62), channel_id=1, source_target_pairs={{0,2},{2,4},{4,6},{6,8},{8,10},{10,12},{12,14},{1,3},{3,5},{5,7},{... | collective-permute-start | bytes 49160 | tf_op jit(solution)/shard_map/ppermute | solution.py:15
  25.8 7.1 %collective-permute-start.8 = (f32[2,8,2,128]{3,2,1,0:T(2,128)S(1)}, f32[2,8,2,128]{3,2,1,0:T(2,128)S(1)}, u32[]{:S(2)}, u32[]{:S(2)}) collective-permute-start(f32[2,8,2,128]{3,2,1,0:T(2,128)S(1)} %get-tuple-element.63), channel_id=1, source_target_pairs={{2,0},{4,2},{6,4},{8,6},{10,8},{12,10},{14,12},{3,1},{5,3},{7,5},{... | collective-permute-start | bytes 49160 | tf_op jit(solution)/shard_map/ppermute | solution.py:17
  33.6 0.6 copy-start.16
  33.7 0.7 copy-start.18
  38.8 15.9 %collective-permute-start.5 = (f32[9,8,16,2]{2,1,3,0:T(8,128)}, f32[9,8,16,2]{2,1,3,0:T(8,128)}, u32[]{:S(2)}, u32[]{:S(2)}) collective-permute-start(f32[9,8,16,2]{2,1,3,0:T(8,128)} %copy.101), channel_id=1, source_target_pairs={{0,16},{16,32},{32,48},{48,64},{64,80},{80,96},{96,112},{112,128},... | collective-permute-start | bytes 27656 | tf_op jit(solution)/shard_map/ppermute | solution.py:15
  41.0 15.9 %collective-permute-start.6 = (f32[9,8,16,2]{2,1,3,0:T(8,128)}, f32[9,8,16,2]{2,1,3,0:T(8,128)}, u32[]{:S(2)}, u32[]{:S(2)}) collective-permute-start(f32[9,8,16,2]{2,1,3,0:T(8,128)} %copy.102), channel_id=1, source_target_pairs={{16,0},{32,16},{48,32},{64,48},{80,64},{96,80},{112,96},{128,112},... | collective-permute-start | bytes 27656 | tf_op jit(solution)/shard_map/ppermute | solution.py:17
  45.8 15.5 %collective-permute-start.9 = (f32[9,8,2,128]{3,1,2,0:T(8,128)}, f32[9,8,2,128]{3,1,2,0:T(8,128)}, u32[]{:S(2)}, u32[]{:S(2)}) collective-permute-start(f32[9,8,2,128]{3,1,2,0:T(8,128)} %copy.105), channel_id=1, source_target_pairs={{0,2},{2,4},{4,6},{6,8},{8,10},{10,12},{12,14},{1,3},{3,5},{5,7},{... | collective-permute-start | bytes 221192 | tf_op jit(solution)/shard_map/ppermute | solution.py:15
  48.5 13.8 %collective-permute-start.10 = (f32[9,8,2,128]{3,1,2,0:T(8,128)}, f32[9,8,2,128]{3,1,2,0:T(8,128)}, u32[]{:S(2)}, u32[]{:S(2)}) collective-permute-start(f32[9,8,2,128]{3,1,2,0:T(8,128)} %copy.106), channel_id=1, source_target_pairs={{2,0},{4,2},{6,4},{8,6},{10,8},{12,10},{14,12},{3,1},{5,3},{7,5},{... | collective-permute-start | bytes 221192 | tf_op jit(solution)/shard_map/ppermute | solution.py:17
  61.3 2.1 %copy-start.2 = (f32[8,19,128]{2,1,0:T(8,128)S(1)}, f32[8,19,128]{2,1,0:T(8,128)}, u32[]{:S(2)}) copy-start(f32[8,19,128]{2,1,0:T(8,128)} %get-tuple-element.58) | copy-start | bytes 233476
  61.4 2.1 %copy-start.5 = (f32[8,19,128]{2,1,0:T(8,128)S(1)}, f32[8,19,128]{2,1,0:T(8,128)}, u32[]{:S(2)}) copy-start(f32[8,19,128]{2,1,0:T(8,128)} %get-tuple-element.59) | copy-start | bytes 233476
  63.5 0.9 copy-start.17
  63.5 0.9 copy-start.19
  64.4 0.8 copy-start.30
  64.4 1.0 copy-start.28
  65.2 0.7 copy-start.26
  65.4 0.7 copy-start.24
  66.0 2.9 %copy-start.32 = (f32[9]{0:T(128)S(1)}, f32[9]{0:T(128)}, u32[]{:S(2)}) copy-start(f32[9]{0:T(128)} %param.19) | copy-start | bytes 112
  66.1 2.9 %copy-start.33 = (f32[8]{0:T(128)S(1)}, f32[8]{0:T(128)}, u32[]{:S(2)}) copy-start(f32[8]{0:T(128)} %dynamic_slice.11) | copy-start | bytes 100
  66.1 2.9 %copy-start.22 = (s32[16,128]{1,0:T(8,128)S(1)}, s32[16,128]{1,0:T(8,128)}, u32[]{:S(2)}) copy-start(s32[16,128]{1,0:T(8,128)} %param.21) | copy-start | bytes 24580
  66.3 2.7 %collective-permute-start.11 = (f32[9,1,16,128]{3,2,1,0:T(8,128)S(1)}, f32[9,1,16,128]{3,2,1,0:T(8,128)S(1)}, u32[]{:S(2)}, u32[]{:S(2)}) collective-permute-start(f32[9,1,16,128]{3,2,1,0:T(8,128)S(1)} %get-tuple-element.48), channel_id=1, source_target_pairs={{0,1},{2,3},{4,5},{6,7},{8,9},{10,11},{12,13},{14,15},{16,17},{18,... | collective-permute-start | bytes 221192 | tf_op jit(solution)/shard_map/ppermute | solution.py:15
  67.6 3.2 %collective-permute-start.12 = (f32[9,1,16,128]{3,2,1,0:T(8,128)S(1)}, f32[9,1,16,128]{3,2,1,0:T(8,128)S(1)}, u32[]{:S(2)}, u32[]{:S(2)}) collective-permute-start(f32[9,1,16,128]{3,2,1,0:T(8,128)S(1)} %get-tuple-element.49), channel_id=1, source_target_pairs={{1,0},{3,2},{5,4},{7,6},{9,8},{11,10},{13,12},{15,14},{17,16},{19,... | collective-permute-start | bytes 221192 | tf_op jit(solution)/shard_map/ppermute | solution.py:17
  69.0 3.2 %copy-start.9 = (f32[9,1,16,128]{3,2,1,0:T(8,128)}, f32[9,1,16,128]{3,2,1,0:T(8,128)S(1)}, u32[]{:S(2)}) copy-start(f32[9,1,16,128]{3,2,1,0:T(8,128)S(1)} %collective-permute-done.11) | copy-start | bytes 221188
  70.8 1.5 %copy-start.11 = (f32[9,1,16,128]{3,2,1,0:T(8,128)}, f32[9,1,16,128]{3,2,1,0:T(8,128)S(1)}, u32[]{:S(2)}) copy-start(f32[9,1,16,128]{3,2,1,0:T(8,128)S(1)} %collective-permute-done.12) | copy-start | bytes 221188
  74.4 16.1 %collective-permute-start.13 = (f32[9,8,16,2]{2,1,3,0:T(8,128)}, f32[9,8,16,2]{2,1,3,0:T(8,128)}, u32[]{:S(2)}, u32[]{:S(2)}) collective-permute-start(f32[9,8,16,2]{2,1,3,0:T(8,128)} %copy.109), channel_id=1, source_target_pairs={{0,16},{16,32},{32,48},{48,64},{64,80},{80,96},{96,112},{112,128},... | collective-permute-start | bytes 27656 | tf_op jit(solution)/shard_map/ppermute | solution.py:15
  76.6 16.1 %collective-permute-start.14 = (f32[9,8,16,2]{2,1,3,0:T(8,128)}, f32[9,8,16,2]{2,1,3,0:T(8,128)}, u32[]{:S(2)}, u32[]{:S(2)}) collective-permute-start(f32[9,8,16,2]{2,1,3,0:T(8,128)} %copy.110), channel_id=1, source_target_pairs={{16,0},{32,16},{48,32},{64,48},{80,64},{96,80},{112,96},{128,112},... | collective-permute-start | bytes 27656 | tf_op jit(solution)/shard_map/ppermute | solution.py:17
  81.4 15.8 %collective-permute-start.15 = (f32[9,8,2,128]{3,1,2,0:T(8,128)}, f32[9,8,2,128]{3,1,2,0:T(8,128)}, u32[]{:S(2)}, u32[]{:S(2)}) collective-permute-start(f32[9,8,2,128]{3,1,2,0:T(8,128)} %copy.113), channel_id=1, source_target_pairs={{0,2},{2,4},{4,6},{6,8},{8,10},{10,12},{12,14},{1,3},{3,5},{5,7},{... | collective-permute-start | bytes 221192 | tf_op jit(solution)/shard_map/ppermute | solution.py:15
  84.0 14.2 %collective-permute-start.16 = (f32[9,8,2,128]{3,1,2,0:T(8,128)}, f32[9,8,2,128]{3,1,2,0:T(8,128)}, u32[]{:S(2)}, u32[]{:S(2)}) collective-permute-start(f32[9,8,2,128]{3,1,2,0:T(8,128)} %copy.114), channel_id=1, source_target_pairs={{2,0},{4,2},{6,4},{8,6},{10,8},{12,10},{14,12},{3,1},{5,3},{7,5},{... | collective-permute-start | bytes 221192 | tf_op jit(solution)/shard_map/ppermute | solution.py:17
  97.1 2.1 %copy-start.3 = (f32[8,19,128]{2,1,0:T(8,128)S(1)}, f32[8,19,128]{2,1,0:T(8,128)}, u32[]{:S(2)}) copy-start(f32[8,19,128]{2,1,0:T(8,128)} %get-tuple-element.58) | copy-start | bytes 233476
  97.2 2.1 %copy-start.6 = (f32[8,19,128]{2,1,0:T(8,128)S(1)}, f32[8,19,128]{2,1,0:T(8,128)}, u32[]{:S(2)}) copy-start(f32[8,19,128]{2,1,0:T(8,128)} %get-tuple-element.59) | copy-start | bytes 233476
  99.2 0.9 copy-start.10
  99.3 0.9 copy-start.12
  102.1 0.9 copy-start.15
  102.1 0.9 copy-start.14
  102.1 0.9 copy-start.13
  103.2 7.6 %collective-permute-start.17 = (f32[9,1,16,128]{3,2,1,0:T(8,128)S(1)}, f32[9,1,16,128]{3,2,1,0:T(8,128)S(1)}, u32[]{:S(2)}, u32[]{:S(2)}) collective-permute-start(f32[9,1,16,128]{3,2,1,0:T(8,128)S(1)} %get-tuple-element.42), channel_id=1, source_target_pairs={{0,1},{2,3},{4,5},{6,7},{8,9},{10,11},{12,13},{14,15},{16,17},{18,... | collective-permute-start | bytes 221192 | tf_op jit(solution)/shard_map/ppermute | solution.py:15
  104.5 6.3 %collective-permute-start.18 = (f32[9,1,16,128]{3,2,1,0:T(8,128)S(1)}, f32[9,1,16,128]{3,2,1,0:T(8,128)S(1)}, u32[]{:S(2)}, u32[]{:S(2)}) collective-permute-start(f32[9,1,16,128]{3,2,1,0:T(8,128)S(1)} %get-tuple-element.43), channel_id=1, source_target_pairs={{1,0},{3,2},{5,4},{7,6},{9,8},{11,10},{13,12},{15,14},{17,16},{19,... | collective-permute-start | bytes 221192 | tf_op jit(solution)/shard_map/ppermute | solution.py:17
  111.7 13.1 %collective-permute-start.19 = (f32[9,8,16,2]{2,1,3,0:T(8,128)S(1)}, f32[9,8,16,2]{2,1,3,0:T(8,128)S(1)}, u32[]{:S(2)}, u32[]{:S(2)}) collective-permute-start(f32[9,8,16,2]{2,1,3,0:T(8,128)S(1)} %copy.117), channel_id=1, source_target_pairs={{0,16},{16,32},{32,48},{48,64},{64,80},{80,96},{96,112},{112,128},... | collective-permute-start | bytes 27656 | tf_op jit(solution)/shard_map/ppermute | solution.py:15
  112.3 13.0 %collective-permute-start.20 = (f32[9,8,16,2]{2,1,3,0:T(8,128)S(1)}, f32[9,8,16,2]{2,1,3,0:T(8,128)}, u32[]{:S(2)}, u32[]{:S(2)}) collective-permute-start(f32[9,8,16,2]{2,1,3,0:T(8,128)S(1)} %copy.118), channel_id=1, source_target_pairs={{16,0},{32,16},{48,32},{64,48},{80,64},{96,80},{112,96},{128,112},... | collective-permute-start | bytes 27656 | tf_op jit(solution)/shard_map/ppermute | solution.py:17
  116.5 11.1 %collective-permute-start.21 = (f32[9,8,2,128]{3,1,2,0:T(8,128)S(1)}, f32[9,8,2,128]{3,1,2,0:T(8,128)S(1)}, u32[]{:S(2)}, u32[]{:S(2)}) collective-permute-start(f32[9,8,2,128]{3,1,2,0:T(8,128)S(1)} %copy.121), channel_id=1, source_target_pairs={{0,2},{2,4},{4,6},{6,8},{8,10},{10,12},{12,14},{1,3},{3,5},{5,7},{... | collective-permute-start | bytes 221192 | tf_op jit(solution)/shard_map/ppermute | solution.py:15
  118.5 9.3 %collective-permute-start.22 = (f32[9,8,2,128]{3,1,2,0:T(8,128)S(1)}, f32[9,8,2,128]{3,1,2,0:T(8,128)S(1)}, u32[]{:S(2)}, u32[]{:S(2)}) collective-permute-start(f32[9,8,2,128]{3,1,2,0:T(8,128)S(1)} %copy.122), channel_id=1, source_target_pairs={{2,0},{4,2},{6,4},{8,6},{10,8},{12,10},{14,12},{3,1},{5,3},{7,5},{... | collective-permute-start | bytes 221192 | tf_op jit(solution)/shard_map/ppermute | solution.py:17
  127.7 0.9 copy-start.4
  127.7 0.9 copy-start.7
where the time goes:
time: 132 us; the launch traced here: 130 us
  starting transfers between devices  63.9 us (48%)
  local copies, waits for them, and re-layouts  35.3 us (27%)
  other arithmetic  17.8 us (13%)
  waiting for transfers between devices  6.55 us (5%)
  blocking collectives  4.97 us (4%)
  between operations  1.63 us (1%)
    ppermute x11, starting transfers between devices, with_halo(): lax.ppermute(head, axis, [((i + 1) % count, i) for i in range(ends)])  44 us
    ppermute x12, starting transfers between devices, with_halo(): lax.ppermute(tail, axis, [(i, (i + 1) % count) for i in range(ends)])  19.9 us
    slice x16, local copies, waits for them, and re-layouts, with_halo(): lax.slice_in_dim(cells, cells.shape[dim] - width, cells.shape[dim], axis=...  9.57 us
    ppermute x6, local copies, waits for them, and re-layouts, with_halo(): lax.ppermute(head, axis, [((i + 1) % count, i) for i in range(ends)])  7.63 us
    ppermute x6, local copies, waits for them, and re-layouts, with_halo(): lax.ppermute(tail, axis, [(i, (i + 1) % count) for i in range(ends)])  6.89 us
    slice x6, local copies, waits for them, and re-layouts, with_halo(): head = lax.slice_in_dim(cells, 0, width, axis=dim)  6.14 us
    psum x1, blocking collectives, run_split(): emis_grad = lax.psum(emis_grad, 'lev')  4.97 us
    ppermute x11, waiting for transfers between devices, with_halo(): lax.ppermute(head, axis, [((i + 1) % count, i) for i in range(ends)])  4.71 us
  transfers between devices with their start and end apart: 23, of which 3 were waited for; matrix products, arithmetic and copies ran while one was open for 22% of the time, Pallas kernels for 0%

commit v1 on v0

--- a/solution.py
+++ b/solution.py
@@ -143,7 +143,8 @@
             + transport(lon_pad, east_pad, 3, col_count)
             + transport(lat_pad, north_pad, 2, row_count)
         )
-    emis_grad = lax.psum(emis_grad, "lev")
+    blocks = lax.all_gather(emis_grad, "lev")
+    emis_grad = jnp.sum(blocks, axis=0)
     return (adjoint, emis_grad)
 
 

time: 132 us -> 130 us (0.985)
  blocking collectives: 4.97 us -> 2.62 us
    psum x1 -> x0, blocking collectives: 4.97 us -> none  [run_split(): emis_grad = lax.psum(emis_grad, 'lev')]
    all_gather x0 -> x1, blocking collectives: none -> 2.62 us  [run_split(): blocks = lax.all_gather(emis_grad, 'lev')]
  transfers between devices with their start and end apart: 23 -> 23, of which waited for: 3 -> 3; matrix products, arithmetic and copies ran while one was open for 22% -> 23% of each run, Pallas kernels for 0% -> 0%
where the time goes in v1:
time: 130 us; the launch traced here: 129 us
  starting transfers between devices  63.9 us (49%)
  local copies, waits for them, and re-layouts  35.3 us (27%)
  other arithmetic  18.4 us (14%)
  waiting for transfers between devices  6.55 us (5%)
  blocking collectives  2.62 us (2%)
  between operations  1.63 us (1%)
    ppermute x11, starting transfers between devices, with_halo(): lax.ppermute(head, axis, [((i + 1) % count, i) for i in range(ends)])  44 us
    ppermute x12, starting transfers between devices, with_halo(): lax.ppermute(tail, axis, [(i, (i + 1) % count) for i in range(ends)])  19.9 us
    slice x16, local copies, waits for them, and re-layouts, with_halo(): lax.slice_in_dim(cells, cells.shape[dim] - width, cells.shape[dim], axis=...  9.57 us
    ppermute x6, local copies, waits for them, and re-layouts, with_halo(): lax.ppermute(head, axis, [((i + 1) % count, i) for i in range(ends)])  7.63 us
    ppermute x6, local copies, waits for them, and re-layouts, with_halo(): lax.ppermute(tail, axis, [(i, (i + 1) % count) for i in range(ends)])  6.89 us
    slice x6, local copies, waits for them, and re-layouts, with_halo(): head = lax.slice_in_dim(cells, 0, width, axis=dim)  6.14 us
    ppermute x11, waiting for transfers between devices, with_halo(): lax.ppermute(head, axis, [((i + 1) % count, i) for i in range(ends)])  4.71 us
    concatenate x6, other arithmetic, with_halo(): jnp.concatenate([lax.ppermute(tail, axis, [(i, (i + 1) % count) for i in...  4.52 us
  transfers between devices with their start and end apart: 23, of which 3 were waited for; matrix products, arithmetic and copies ran while one was open for 23% of the time, Pallas kernels for 0%

profile of v1, /device:TPU:6, one launch (start us, length us, event | category | flops | bytes accessed | tf_op | source)
XLA Modules:
  0.0 128.6 jit_solution(3179335030440893537)
XLA Ops:
  0.7 0.8 constant_dynamic-slice_fusion
  1.5 1.4 %slice_convert_fusion = (f32[1,9,8,16,128]{4,3,2,1,0:T(8,128)S(1)}, f32[1,9,8,16,128]{4,3,2,1,0:T(8,128)S(1)}, f32[1,9,8,16,128]{4,3,2,1,0:T(8,128)S(1)}) fusion(bf16[3,9,8,16,128]{4,3,2,1,0:T(8,128)(2,1)} %param.12), kind=kLoop, calls=%fused_computation.97 | loop fusion | flops 442368 | bytes 2654208 | tf_op jit(solution)/shard_map/convert_element_type | solution.py:138
  3.8 0.7 fusion.59
  4.4 1.7 %collective-permute-start.1 = (f32[9,1,16,128]{3,2,1,0:T(8,128)}, f32[9,1,16,128]{3,2,1,0:T(8,128)S(1)}, u32[]{:S(2)}, u32[]{:S(2)}) collective-permute-start(f32[9,1,16,128]{3,2,1,0:T(8,128)} %get-tuple-element.52), channel_id=1, source_target_pairs={{0,1},{2,3},{4,5},{6,7},{8,9},{10,11},{12,13},{14,15},{16,17},{18,... | collective-permute-start | bytes 221192 | tf_op jit(solution)/shard_map/ppermute | solution.py:15
  6.2 1.3 %collective-permute-start.2 = (f32[9,1,16,128]{3,2,1,0:T(8,128)}, f32[9,1,16,128]{3,2,1,0:T(8,128)S(1)}, u32[]{:S(2)}, u32[]{:S(2)}) collective-permute-start(f32[9,1,16,128]{3,2,1,0:T(8,128)} %get-tuple-element.53), channel_id=1, source_target_pairs={{1,0},{3,2},{5,4},{7,6},{9,8},{11,10},{13,12},{15,14},{17,16},{19,... | collective-permute-start | bytes 221192 | tf_op jit(solution)/shard_map/ppermute | solution.py:17
  7.6 3.0 %collective-permute-start = (f32[1,1,16,128]{3,2,1,0:T(8,128)S(1)}, f32[1,1,16,128]{3,2,1,0:T(8,128)S(1)}, u32[]{:S(2)}, u32[]{:S(2)}) collective-permute-start(f32[1,1,16,128]{3,2,1,0:T(8,128)S(1)} %slice.569), channel_id=1, source_target_pairs={{0,1},{2,3},{4,5},{6,7},{8,9},{10,11},{12,13},{14,15},{16,17},{18,... | collective-permute-start | bytes 24584 | tf_op jit(solution)/shard_map/ppermute | solution.py:15
  10.8 1.7 %collective-permute-start.3 = (f32[2,8,16,2]{3,2,1,0:T(8,128)S(1)}, f32[2,8,16,2]{3,2,1,0:T(8,128)S(1)}, u32[]{:S(2)}, u32[]{:S(2)}) collective-permute-start(f32[2,8,16,2]{3,2,1,0:T(8,128)S(1)} %get-tuple-element.58), channel_id=1, source_target_pairs={{0,16},{16,32},{32,48},{48,64},{64,80},{80,96},{96,112},{112,128},... | collective-permute-start | bytes 6152 | tf_op jit(solution)/shard_map/ppermute | solution.py:15
  12.5 5.4 %collective-permute-start.4 = (f32[2,8,16,2]{3,2,1,0:T(8,128)S(1)}, f32[2,8,16,2]{3,2,1,0:T(8,128)S(1)}, u32[]{:S(2)}, u32[]{:S(2)}) collective-permute-start(f32[2,8,16,2]{3,2,1,0:T(8,128)S(1)} %get-tuple-element.59), channel_id=1, source_target_pairs={{16,0},{32,16},{48,32},{64,48},{80,64},{96,80},{112,96},{128,112},... | collective-permute-start | bytes 6152 | tf_op jit(solution)/shard_map/ppermute | solution.py:17
  18.4 0.7 dynamic_slice.11
  19.0 1.8 %collective-permute-done.3 = f32[2,8,16,2]{3,2,1,0:T(8,128)S(1)} collective-permute-done((f32[2,8,16,2]{3,2,1,0:T(8,128)S(1)}, f32[2,8,16,2]{3,2,1,0:T(8,128)S(1)}, u32[]{:S(2)}, u32[]{:S(2)}) %collective-permute-start.3) | collective-permute-done | bytes 2080 | tf_op jit(solution)/shard_map/ppermute | solution.py:15
  20.8 4.9 %collective-permute-start.7 = (f32[2,8,2,128]{3,2,1,0:T(2,128)S(1)}, f32[2,8,2,128]{3,2,1,0:T(2,128)S(1)}, u32[]{:S(2)}, u32[]{:S(2)}) collective-permute-start(f32[2,8,2,128]{3,2,1,0:T(2,128)S(1)} %get-tuple-element.60), channel_id=1, source_target_pairs={{0,2},{2,4},{4,6},{6,8},{8,10},{10,12},{12,14},{1,3},{3,5},{5,7},{... | collective-permute-start | bytes 49160 | tf_op jit(solution)/shard_map/ppermute | solution.py:15
  25.8 3.3 %collective-permute-start.8 = (f32[2,8,2,128]{3,2,1,0:T(2,128)S(1)}, f32[2,8,2,128]{3,2,1,0:T(2,128)S(1)}, u32[]{:S(2)}, u32[]{:S(2)}) collective-permute-start(f32[2,8,2,128]{3,2,1,0:T(2,128)S(1)} %get-tuple-element.61), channel_id=1, source_target_pairs={{2,0},{4,2},{6,4},{8,6},{10,8},{12,10},{14,12},{3,1},{5,3},{7,5},{... | collective-permute-start | bytes 49160 | tf_op jit(solution)/shard_map/ppermute | solution.py:17
  29.2 0.7 fusion.35
  30.0 2.9 %collective-permute-done.8 = f32[2,8,2,128]{3,2,1,0:T(2,128)S(1)} collective-permute-done((f32[2,8,2,128]{3,2,1,0:T(2,128)S(1)}, f32[2,8,2,128]{3,2,1,0:T(2,128)S(1)}, u32[]{:S(2)}, u32[]{:S(2)}) %collective-permute-start.8) | collective-permute-done | bytes 16416 | tf_op jit(solution)/shard_map/ppermute | solution.py:17
  32.9 0.7 maximum_bitcast_fusion.1
  33.7 0.6 copy-done.16
  34.3 1.1 fusion.1
  35.5 1.2 fusion.57
  36.6 2.2 %copy.101 = f32[9,8,16,2]{2,1,3,0:T(8,128)} copy(f32[9,8,16,2]{3,2,1,0:T(8,128)} %get-tuple-element.48) | data formatting | bytes 18432 | tf_op jit(solution)/shard_map/slice | solution.py:12
  38.8 2.2 %copy.102 = f32[9,8,16,2]{2,1,3,0:T(8,128)} copy(f32[9,8,16,2]{3,2,1,0:T(8,128)} %get-tuple-element.49) | data formatting | bytes 18432 | tf_op jit(solution)/shard_map/slice | solution.py:11
  41.0 4.1 %collective-permute-start.6 = (f32[9,8,16,2]{2,1,3,0:T(8,128)}, f32[9,8,16,2]{2,1,3,0:T(8,128)}, u32[]{:S(2)}, u32[]{:S(2)}) collective-permute-start(f32[9,8,16,2]{2,1,3,0:T(8,128)} %copy.102), channel_id=1, source_target_pairs={{16,0},{32,16},{48,32},{64,48},{80,64},{96,80},{112,96},{128,112},... | collective-permute-start | bytes 27656 | tf_op jit(solution)/shard_map/ppermute | solution.py:17
  45.2 0.6 copy.105
  45.8 2.0 %collective-permute-start.9 = (f32[9,8,2,128]{3,1,2,0:T(8,128)}, f32[9,8,2,128]{3,1,2,0:T(8,128)}, u32[]{:S(2)}, u32[]{:S(2)}) collective-permute-start(f32[9,8,2,128]{3,1,2,0:T(8,128)} %copy.105), channel_id=1, source_target_pairs={{0,2},{2,4},{4,6},{6,8},{8,10},{10,12},{12,14},{1,3},{3,5},{5,7},{... | collective-permute-start | bytes 221192 | tf_op jit(solution)/shard_map/ppermute | solution.py:15
  47.9 0.6 copy.106
  48.5 6.2 %collective-permute-start.10 = (f32[9,8,2,128]{3,1,2,0:T(8,128)}, f32[9,8,2,128]{3,1,2,0:T(8,128)}, u32[]{:S(2)}, u32[]{:S(2)}) collective-permute-start(f32[9,8,2,128]{3,1,2,0:T(8,128)} %copy.106), channel_id=1, source_target_pairs={{2,0},{4,2},{6,4},{8,6},{10,8},{12,10},{14,12},{3,1},{5,3},{7,5},{... | collective-permute-start | bytes 221192 | tf_op jit(solution)/shard_map/ppermute | solution.py:17
  54.7 2.2 %copy.103 = f32[9,8,16,2]{3,2,1,0:T(8,128)} copy(f32[9,8,16,2]{2,1,3,0:T(8,128)} %collective-permute-done.5) | data formatting | bytes 18432 | tf_op jit(solution)/shard_map/ppermute | solution.py:15
  56.9 2.2 %copy.104 = f32[9,8,16,2]{3,2,1,0:T(8,128)} copy(f32[9,8,16,2]{2,1,3,0:T(8,128)} %collective-permute-done.6) | data formatting | bytes 18432 | tf_op jit(solution)/shard_map/ppermute | solution.py:17
  59.1 1.8 %pad_maximum_fusion = f32[9,8,16,132]{3,2,1,0:T(8,128)S(1)} fusion(f32[9,8,16,2]{3,2,1,0:T(8,128)} %copy.104, f32[9,8,16,128]{3,2,1,0:T(8,128)S(1)} %fusion.1, f32[9,8,16,2]{3,2,1,0:T(8,128)} %copy.103), kind=kLoop, calls=%fused_computation.3 | loop fusion | flops 304128 | bytes 1216512 | tf_op jit(solution)/shard_map/concatenate | solution.py:13
  61.4 1.0 copy.107
  62.4 0.9 copy.108
  63.7 0.7 copy-done.17
  64.4 0.7 fusion.25
  66.3 1.3 %collective-permute-start.11 = (f32[9,1,16,128]{3,2,1,0:T(8,128)S(1)}, f32[9,1,16,128]{3,2,1,0:T(8,128)S(1)}, u32[]{:S(2)}, u32[]{:S(2)}) collective-permute-start(f32[9,1,16,128]{3,2,1,0:T(8,128)S(1)} %get-tuple-element.46), channel_id=1, source_target_pairs={{0,1},{2,3},{4,5},{6,7},{8,9},{10,11},{12,13},{14,15},{16,17},{18,... | collective-permute-start | bytes 221192 | tf_op jit(solution)/shard_map/ppermute | solution.py:15
  67.6 1.3 %collective-permute-start.12 = (f32[9,1,16,128]{3,2,1,0:T(8,128)S(1)}, f32[9,1,16,128]{3,2,1,0:T(8,128)S(1)}, u32[]{:S(2)}, u32[]{:S(2)}) collective-permute-start(f32[9,1,16,128]{3,2,1,0:T(8,128)S(1)} %get-tuple-element.47), channel_id=1, source_target_pairs={{1,0},{3,2},{5,4},{7,6},{9,8},{11,10},{13,12},{15,14},{17,16},{19,... | collective-permute-start | bytes 221192 | tf_op jit(solution)/shard_map/ppermute | solution.py:17
  69.0 1.7 %collective-permute-done.12 = f32[9,1,16,128]{3,2,1,0:T(8,128)S(1)} collective-permute-done((f32[9,1,16,128]{3,2,1,0:T(8,128)S(1)}, f32[9,1,16,128]{3,2,1,0:T(8,128)S(1)}, u32[]{:S(2)}, u32[]{:S(2)}) %collective-permute-start.12) | collective-permute-done | bytes 73760 | tf_op jit(solution)/shard_map/ppermute | solution.py:17
  71.0 1.2 fusion.54
  72.2 2.2 %copy.109 = f32[9,8,16,2]{2,1,3,0:T(8,128)} copy(f32[9,8,16,2]{3,2,1,0:T(8,128)} %get-tuple-element.42) | data formatting | bytes 18432 | tf_op jit(solution)/shard_map/slice | solution.py:12
  74.4 2.2 %copy.110 = f32[9,8,16,2]{2,1,3,0:T(8,128)} copy(f32[9,8,16,2]{3,2,1,0:T(8,128)} %get-tuple-element.43) | data formatting | bytes 18432 | tf_op jit(solution)/shard_map/slice | solution.py:11
  76.6 4.1 %collective-permute-start.14 = (f32[9,8,16,2]{2,1,3,0:T(8,128)}, f32[9,8,16,2]{2,1,3,0:T(8,128)}, u32[]{:S(2)}, u32[]{:S(2)}) collective-permute-start(f32[9,8,16,2]{2,1,3,0:T(8,128)} %copy.110), channel_id=1, source_target_pairs={{16,0},{32,16},{48,32},{64,48},{80,64},{96,80},{112,96},{128,112},... | collective-permute-start | bytes 27656 | tf_op jit(solution)/shard_map/ppermute | solution.py:17
  80.8 0.6 copy.113
  81.4 1.9 %collective-permute-start.15 = (f32[9,8,2,128]{3,1,2,0:T(8,128)}, f32[9,8,2,128]{3,1,2,0:T(8,128)}, u32[]{:S(2)}, u32[]{:S(2)}) collective-permute-start(f32[9,8,2,128]{3,1,2,0:T(8,128)} %copy.113), channel_id=1, source_target_pairs={{0,2},{2,4},{4,6},{6,8},{8,10},{10,12},{12,14},{1,3},{3,5},{5,7},{... | collective-permute-start | bytes 221192 | tf_op jit(solution)/shard_map/ppermute | solution.py:15
  83.3 0.6 copy.114
  84.0 6.5 %collective-permute-start.16 = (f32[9,8,2,128]{3,1,2,0:T(8,128)}, f32[9,8,2,128]{3,1,2,0:T(8,128)}, u32[]{:S(2)}, u32[]{:S(2)}) collective-permute-start(f32[9,8,2,128]{3,1,2,0:T(8,128)} %copy.114), channel_id=1, source_target_pairs={{2,0},{4,2},{6,4},{8,6},{10,8},{12,10},{14,12},{3,1},{5,3},{7,5},{... | collective-permute-start | bytes 221192 | tf_op jit(solution)/shard_map/ppermute | solution.py:17
  90.5 2.2 %copy.111 = f32[9,8,16,2]{3,2,1,0:T(8,128)} copy(f32[9,8,16,2]{2,1,3,0:T(8,128)} %collective-permute-done.13) | data formatting | bytes 18432 | tf_op jit(solution)/shard_map/ppermute | solution.py:15
  92.7 2.2 %copy.112 = f32[9,8,16,2]{3,2,1,0:T(8,128)} copy(f32[9,8,16,2]{2,1,3,0:T(8,128)} %collective-permute-done.14) | data formatting | bytes 18432 | tf_op jit(solution)/shard_map/ppermute | solution.py:17
  94.9 1.8 %pad_maximum_fusion.1 = f32[9,8,16,132]{3,2,1,0:T(8,128)S(1)} fusion(f32[9,8,16,2]{3,2,1,0:T(8,128)} %copy.112, f32[9,8,16,128]{3,2,1,0:T(8,128)S(1)} %fusion.3, f32[9,8,16,2]{3,2,1,0:T(8,128)} %copy.111), kind=kLoop, calls=%fused_computation.4 | loop fusion | flops 304128 | bytes 1216512 | tf_op jit(solution)/shard_map/concatenate | solution.py:13
  97.2 1.0 copy.115
  98.2 0.9 copy.116
  99.5 0.6 copy-done.10
  100.2 1.6 %multiply_reduce_fusion.1 = (f32[9,16,128]{2,1,0:T(8,128)}, f32[9,16,128]{2,1,0:T(8,128)}, f32[9,16,128]{2,1,0:T(8,128)}, f32[9,8,16,128]{3,2,1,0:T(8,128)S(1)}) fusion(f32[9,8,16,128]{3,2,1,0:T(8,128)S(1)} %fusion.25, f32[9,8]{1,0:T(8,128)S(1)} %broadcast_multiply_fusion.13, f32[9,8,16,128]{3,2,1,0:T(8,128)S(1)} %copy-done.1, ...), kind=kLoop, calls=%fused_computation.79 | loop fusion | flops 4663296 | bytes 7709248 | tf_op jit(solution)/shard_map/reduce_sum | solution.py:90
  103.2 1.3 %collective-permute-start.17 = (f32[9,1,16,128]{3,2,1,0:T(8,128)S(1)}, f32[9,1,16,128]{3,2,1,0:T(8,128)S(1)}, u32[]{:S(2)}, u32[]{:S(2)}) collective-permute-start(f32[9,1,16,128]{3,2,1,0:T(8,128)S(1)} %get-tuple-element.40), channel_id=1, source_target_pairs={{0,1},{2,3},{4,5},{6,7},{8,9},{10,11},{12,13},{14,15},{16,17},{18,... | collective-permute-start | bytes 221192 | tf_op jit(solution)/shard_map/ppermute | solution.py:15
  104.5 1.3 %collective-permute-start.18 = (f32[9,1,16,128]{3,2,1,0:T(8,128)S(1)}, f32[9,1,16,128]{3,2,1,0:T(8,128)S(1)}, u32[]{:S(2)}, u32[]{:S(2)}) collective-permute-start(f32[9,1,16,128]{3,2,1,0:T(8,128)S(1)} %get-tuple-element.41), channel_id=1, source_target_pairs={{1,0},{3,2},{5,4},{7,6},{9,8},{11,10},{13,12},{15,14},{17,16},{19,... | collective-permute-start | bytes 221192 | tf_op jit(solution)/shard_map/ppermute | solution.py:17
  105.8 2.6 %all_gather.4 = f32[2,3,16,128]{3,2,1,0:T(8,128)S(1)} all-gather(f32[1,3,16,128]{3,2,1,0:T(8,128)S(1)} %bitcast_multiply_fusion), channel_id=1, replica_groups=mesh['lon'=16,'lat'=8,'lev'=2] {'lev'}, dimensions={0}, use_global_device_ids=true | all-gather | bytes 73728 | tf_op jit(solution)/shard_map/all_gather | solution.py:146
  108.4 0.6 reduce_sum.78
  109.5 0.5 copy.117
  110.1 0.5 copy.118
  110.6 4.2 %collective-permute-start.20 = (f32[9,8,16,2]{2,1,3,0:T(8,128)S(1)}, f32[9,8,16,2]{2,1,3,0:T(8,128)}, u32[]{:S(2)}, u32[]{:S(2)}) collective-permute-start(f32[9,8,16,2]{2,1,3,0:T(8,128)S(1)} %copy.118), channel_id=1, source_target_pairs={{16,0},{32,16},{48,32},{64,48},{80,64},{96,80},{112,96},{128,112},... | collective-permute-start | bytes 27656 | tf_op jit(solution)/shard_map/ppermute | solution.py:17
  114.8 1.9 %collective-permute-start.21 = (f32[9,8,2,128]{3,1,2,0:T(8,128)S(1)}, f32[9,8,2,128]{3,1,2,0:T(8,128)S(1)}, u32[]{:S(2)}, u32[]{:S(2)}) collective-permute-start(f32[9,8,2,128]{3,1,2,0:T(8,128)S(1)} %copy.121), channel_id=1, source_target_pairs={{0,2},{2,4},{4,6},{6,8},{8,10},{10,12},{12,14},{1,3},{3,5},{5,7},{... | collective-permute-start | bytes 221192 | tf_op jit(solution)/shard_map/ppermute | solution.py:15
  116.8 6.3 %collective-permute-start.22 = (f32[9,8,2,128]{3,1,2,0:T(8,128)S(1)}, f32[9,8,2,128]{3,1,2,0:T(8,128)S(1)}, u32[]{:S(2)}, u32[]{:S(2)}) collective-permute-start(f32[9,8,2,128]{3,1,2,0:T(8,128)S(1)} %copy.122), channel_id=1, source_target_pairs={{2,0},{4,2},{6,4},{8,6},{10,8},{12,10},{14,12},{3,1},{5,3},{7,5},{... | collective-permute-start | bytes 221192 | tf_op jit(solution)/shard_map/ppermute | solution.py:17
  123.1 0.5 copy.119
  123.6 1.4 %copy.120 = f32[9,8,16,2]{3,2,1,0:T(8,128)S(1)} copy(f32[9,8,16,2]{2,1,3,0:T(8,128)} %collective-permute-done.20) | data formatting | bytes 18432 | tf_op jit(solution)/shard_map/ppermute | solution.py:17
  125.0 0.5 pad_maximum_fusion.2
  126.2 0.6 copy-done.4
  127.1 1.6 %fusion.7 = f32[9,8,16,128]{3,2,1,0:T(8,128)} fusion(f32[9,8,19,128]{3,2,1,0:T(8,128)S(1)} %get-tuple-element.28, f32[9,8,19,128]{3,2,1,0:T(8,128)S(1)} %get-tuple-element.27, f32[9,8,16,131]{3,2,1,0:T(8,128)S(1)} %get-tuple-element.22, f32[9,8,16,131]{3,2,1,0:T(8,128)S(1)} %get-tuple-element.21, f32[8,16,128]{2,1,0:T(8,128)S(1)} %broadcast_select_fusion, ...), kind=kLoop, calls=%fused_computation.23 | loop fusion | flops 3833856 | bytes 6308128 | tf_op jit(solution)/shard_map/add | solution.py:142
  (155 shorter events, 7.8 us)
Async XLA Ops:
  0.6 17.4 %copy-start = (f32[8,9]{1,0:T(8,128)S(1)}, f32[8,9]{1,0:T(8,128)}, u32[]{:S(2)}) copy-start(f32[8,9]{1,0:T(8,128)} %param.16) | copy-start | bytes 868
  1.4 1.5 %copy-start.29 = (f32[8]{0:T(128)}, f32[8]{0:T(128)S(1)}, u32[]{:S(2)}) copy-start(f32[8]{0:T(128)S(1)} %get-tuple-element.68) | copy-start | bytes 100
  1.4 1.7 %copy-start.27 = (f32[8]{0:T(128)}, f32[8]{0:T(128)S(1)}, u32[]{:S(2)}) copy-start(f32[8]{0:T(128)S(1)} %get-tuple-element.67) | copy-start | bytes 100
  1.4 1.6 %copy-start.25 = (f32[8]{0:T(128)}, f32[8]{0:T(128)S(1)}, u32[]{:S(2)}) copy-start(f32[8]{0:T(128)S(1)} %get-tuple-element.74) | copy-start | bytes 100
  1.4 2.0 %copy-start.23 = (f32[8]{0:T(128)}, f32[8]{0:T(128)S(1)}, u32[]{:S(2)}) copy-start(f32[8]{0:T(128)S(1)} %get-tuple-element.73) | copy-start | bytes 100
  1.5 1.4 %copy-start.1 = (f32[9,8,16,128]{3,2,1,0:T(8,128)S(1)}, f32[9,8,16,128]{3,2,1,0:T(8,128)}, u32[]{:S(2)}) copy-start(f32[9,8,16,128]{3,2,1,0:T(8,128)} %param.11) | copy-start | bytes 1769476
  3.6 3.9 %copy-start.8 = (f32[8,16,128]{2,1,0:T(8,128)S(1)}, f32[8,16,128]{2,1,0:T(8,128)}, u32[]{:S(2)}) copy-start(f32[8,16,128]{2,1,0:T(8,128)} %param.14) | copy-start | bytes 196612
  3.6 7.0 %copy-start.20 = (f32[2,8,16,128]{3,2,1,0:T(8,128)S(1)}, f32[2,8,16,128]{3,2,1,0:T(8,128)}, u32[]{:S(2)}) copy-start(f32[2,8,16,128]{3,2,1,0:T(8,128)} %param.13) | copy-start | bytes 393220
  3.6 14.3 %copy-start.21 = (s32[16,128]{1,0:T(8,128)S(1)}, s32[16,128]{1,0:T(8,128)}, u32[]{:S(2)}) copy-start(s32[16,128]{1,0:T(8,128)} %param.20) | copy-start | bytes 24580
  3.6 14.4 %copy-start.34 = (s32[16]{0:T(128)S(1)}, s32[16]{0:T(128)}, u32[]{:S(2)}) copy-start(s32[16]{0:T(128)} %param.17) | copy-start | bytes 196
  3.7 14.6 %copy-start.35 = (f32[16]{0:T(128)S(1)}, f32[16]{0:T(128)}, u32[]{:S(2)}) copy-start(f32[16]{0:T(128)} %param.18) | copy-start | bytes 196
  4.4 29.2 %collective-permute-start.1 = (f32[9,1,16,128]{3,2,1,0:T(8,128)}, f32[9,1,16,128]{3,2,1,0:T(8,128)S(1)}, u32[]{:S(2)}, u32[]{:S(2)}) collective-permute-start(f32[9,1,16,128]{3,2,1,0:T(8,128)} %get-tuple-element.52), channel_id=1, source_target_pairs={{0,1},{2,3},{4,5},{6,7},{8,9},{10,11},{12,13},{14,15},{16,17},{18,... | collective-permute-start | bytes 221192 | tf_op jit(solution)/shard_map/ppermute | solution.py:15
  6.2 27.5 %collective-permute-start.2 = (f32[9,1,16,128]{3,2,1,0:T(8,128)}, f32[9,1,16,128]{3,2,1,0:T(8,128)S(1)}, u32[]{:S(2)}, u32[]{:S(2)}) collective-permute-start(f32[9,1,16,128]{3,2,1,0:T(8,128)} %get-tuple-element.53), channel_id=1, source_target_pairs={{1,0},{3,2},{5,4},{7,6},{9,8},{11,10},{13,12},{15,14},{17,16},{19,... | collective-permute-start | bytes 221192 | tf_op jit(solution)/shard_map/ppermute | solution.py:17
  7.5 10.5 %copy-start.31 = (pred[8]{0:T(512)(128)(4,1)}, pred[8]{0:T(512)(128)(4,1)S(1)}, u32[]{:S(2)}) copy-start(pred[8]{0:T(512)(128)(4,1)S(1)} %fusion.46) | copy-start | bytes 28
  7.6 21.7 %collective-permute-start = (f32[1,1,16,128]{3,2,1,0:T(8,128)S(1)}, f32[1,1,16,128]{3,2,1,0:T(8,128)S(1)}, u32[]{:S(2)}, u32[]{:S(2)}) collective-permute-start(f32[1,1,16,128]{3,2,1,0:T(8,128)S(1)} %slice.569), channel_id=1, source_target_pairs={{0,1},{2,3},{4,5},{6,7},{8,9},{10,11},{12,13},{14,15},{16,17},{18,... | collective-permute-start | bytes 24584 | tf_op jit(solution)/shard_map/ppermute | solution.py:15
  10.8 10.0 %collective-permute-start.3 = (f32[2,8,16,2]{3,2,1,0:T(8,128)S(1)}, f32[2,8,16,2]{3,2,1,0:T(8,128)S(1)}, u32[]{:S(2)}, u32[]{:S(2)}) collective-permute-start(f32[2,8,16,2]{3,2,1,0:T(8,128)S(1)} %get-tuple-element.58), channel_id=1, source_target_pairs={{0,16},{16,32},{32,48},{48,64},{64,80},{80,96},{96,112},{112,128},... | collective-permute-start | bytes 6152 | tf_op jit(solution)/shard_map/ppermute | solution.py:15
  12.5 13.3 %collective-permute-start.4 = (f32[2,8,16,2]{3,2,1,0:T(8,128)S(1)}, f32[2,8,16,2]{3,2,1,0:T(8,128)S(1)}, u32[]{:S(2)}, u32[]{:S(2)}) collective-permute-start(f32[2,8,16,2]{3,2,1,0:T(8,128)S(1)} %get-tuple-element.59), channel_id=1, source_target_pairs={{16,0},{32,16},{48,32},{64,48},{80,64},{96,80},{112,96},{128,112},... | collective-permute-start | bytes 6152 | tf_op jit(solution)/shard_map/ppermute | solution.py:17
  20.8 9.1 %collective-permute-start.7 = (f32[2,8,2,128]{3,2,1,0:T(2,128)S(1)}, f32[2,8,2,128]{3,2,1,0:T(2,128)S(1)}, u32[]{:S(2)}, u32[]{:S(2)}) collective-permute-start(f32[2,8,2,128]{3,2,1,0:T(2,128)S(1)} %get-tuple-element.60), channel_id=1, source_target_pairs={{0,2},{2,4},{4,6},{6,8},{8,10},{10,12},{12,14},{1,3},{3,5},{5,7},{... | collective-permute-start | bytes 49160 | tf_op jit(solution)/shard_map/ppermute | solution.py:15
  25.8 7.1 %collective-permute-start.8 = (f32[2,8,2,128]{3,2,1,0:T(2,128)S(1)}, f32[2,8,2,128]{3,2,1,0:T(2,128)S(1)}, u32[]{:S(2)}, u32[]{:S(2)}) collective-permute-start(f32[2,8,2,128]{3,2,1,0:T(2,128)S(1)} %get-tuple-element.61), channel_id=1, source_target_pairs={{2,0},{4,2},{6,4},{8,6},{10,8},{12,10},{14,12},{3,1},{5,3},{7,5},{... | collective-permute-start | bytes 49160 | tf_op jit(solution)/shard_map/ppermute | solution.py:17
  33.6 0.6 copy-start.16
  33.7 0.7 copy-start.18
  38.8 15.9 %collective-permute-start.5 = (f32[9,8,16,2]{2,1,3,0:T(8,128)}, f32[9,8,16,2]{2,1,3,0:T(8,128)}, u32[]{:S(2)}, u32[]{:S(2)}) collective-permute-start(f32[9,8,16,2]{2,1,3,0:T(8,128)} %copy.101), channel_id=1, source_target_pairs={{0,16},{16,32},{32,48},{48,64},{64,80},{80,96},{96,112},{112,128},... | collective-permute-start | bytes 27656 | tf_op jit(solution)/shard_map/ppermute | solution.py:15
  41.0 15.9 %collective-permute-start.6 = (f32[9,8,16,2]{2,1,3,0:T(8,128)}, f32[9,8,16,2]{2,1,3,0:T(8,128)}, u32[]{:S(2)}, u32[]{:S(2)}) collective-permute-start(f32[9,8,16,2]{2,1,3,0:T(8,128)} %copy.102), channel_id=1, source_target_pairs={{16,0},{32,16},{48,32},{64,48},{80,64},{96,80},{112,96},{128,112},... | collective-permute-start | bytes 27656 | tf_op jit(solution)/shard_map/ppermute | solution.py:17
  45.8 15.5 %collective-permute-start.9 = (f32[9,8,2,128]{3,1,2,0:T(8,128)}, f32[9,8,2,128]{3,1,2,0:T(8,128)}, u32[]{:S(2)}, u32[]{:S(2)}) collective-permute-start(f32[9,8,2,128]{3,1,2,0:T(8,128)} %copy.105), channel_id=1, source_target_pairs={{0,2},{2,4},{4,6},{6,8},{8,10},{10,12},{12,14},{1,3},{3,5},{5,7},{... | collective-permute-start | bytes 221192 | tf_op jit(solution)/shard_map/ppermute | solution.py:15
  48.5 13.8 %collective-permute-start.10 = (f32[9,8,2,128]{3,1,2,0:T(8,128)}, f32[9,8,2,128]{3,1,2,0:T(8,128)}, u32[]{:S(2)}, u32[]{:S(2)}) collective-permute-start(f32[9,8,2,128]{3,1,2,0:T(8,128)} %copy.106), channel_id=1, source_target_pairs={{2,0},{4,2},{6,4},{8,6},{10,8},{12,10},{14,12},{3,1},{5,3},{7,5},{... | collective-permute-start | bytes 221192 | tf_op jit(solution)/shard_map/ppermute | solution.py:17
  61.3 2.1 %copy-start.2 = (f32[8,19,128]{2,1,0:T(8,128)S(1)}, f32[8,19,128]{2,1,0:T(8,128)}, u32[]{:S(2)}) copy-start(f32[8,19,128]{2,1,0:T(8,128)} %get-tuple-element.56) | copy-start | bytes 233476
  61.4 2.1 %copy-start.5 = (f32[8,19,128]{2,1,0:T(8,128)S(1)}, f32[8,19,128]{2,1,0:T(8,128)}, u32[]{:S(2)}) copy-start(f32[8,19,128]{2,1,0:T(8,128)} %get-tuple-element.57) | copy-start | bytes 233476
  63.5 0.9 copy-start.17
  63.5 0.9 copy-start.19
  64.4 0.8 copy-start.30
  64.4 1.0 copy-start.28
  65.2 0.7 copy-start.26
  65.4 0.7 copy-start.24
  66.0 2.9 %copy-start.32 = (f32[9]{0:T(128)S(1)}, f32[9]{0:T(128)}, u32[]{:S(2)}) copy-start(f32[9]{0:T(128)} %param.19) | copy-start | bytes 112
  66.1 2.9 %copy-start.33 = (f32[8]{0:T(128)S(1)}, f32[8]{0:T(128)}, u32[]{:S(2)}) copy-start(f32[8]{0:T(128)} %dynamic_slice.11) | copy-start | bytes 100
  66.1 2.9 %copy-start.22 = (s32[16,128]{1,0:T(8,128)S(1)}, s32[16,128]{1,0:T(8,128)}, u32[]{:S(2)}) copy-start(s32[16,128]{1,0:T(8,128)} %param.21) | copy-start | bytes 24580
  66.3 2.7 %collective-permute-start.11 = (f32[9,1,16,128]{3,2,1,0:T(8,128)S(1)}, f32[9,1,16,128]{3,2,1,0:T(8,128)S(1)}, u32[]{:S(2)}, u32[]{:S(2)}) collective-permute-start(f32[9,1,16,128]{3,2,1,0:T(8,128)S(1)} %get-tuple-element.46), channel_id=1, source_target_pairs={{0,1},{2,3},{4,5},{6,7},{8,9},{10,11},{12,13},{14,15},{16,17},{18,... | collective-permute-start | bytes 221192 | tf_op jit(solution)/shard_map/ppermute | solution.py:15
  67.6 3.2 %collective-permute-start.12 = (f32[9,1,16,128]{3,2,1,0:T(8,128)S(1)}, f32[9,1,16,128]{3,2,1,0:T(8,128)S(1)}, u32[]{:S(2)}, u32[]{:S(2)}) collective-permute-start(f32[9,1,16,128]{3,2,1,0:T(8,128)S(1)} %get-tuple-element.47), channel_id=1, source_target_pairs={{1,0},{3,2},{5,4},{7,6},{9,8},{11,10},{13,12},{15,14},{17,16},{19,... | collective-permute-start | bytes 221192 | tf_op jit(solution)/shard_map/ppermute | solution.py:17
  69.0 3.2 %copy-start.9 = (f32[9,1,16,128]{3,2,1,0:T(8,128)}, f32[9,1,16,128]{3,2,1,0:T(8,128)S(1)}, u32[]{:S(2)}) copy-start(f32[9,1,16,128]{3,2,1,0:T(8,128)S(1)} %collective-permute-done.11) | copy-start | bytes 221188
  70.8 1.5 %copy-start.11 = (f32[9,1,16,128]{3,2,1,0:T(8,128)}, f32[9,1,16,128]{3,2,1,0:T(8,128)S(1)}, u32[]{:S(2)}) copy-start(f32[9,1,16,128]{3,2,1,0:T(8,128)S(1)} %collective-permute-done.12) | copy-start | bytes 221188
  74.4 16.1 %collective-permute-start.13 = (f32[9,8,16,2]{2,1,3,0:T(8,128)}, f32[9,8,16,2]{2,1,3,0:T(8,128)}, u32[]{:S(2)}, u32[]{:S(2)}) collective-permute-start(f32[9,8,16,2]{2,1,3,0:T(8,128)} %copy.109), channel_id=1, source_target_pairs={{0,16},{16,32},{32,48},{48,64},{64,80},{80,96},{96,112},{112,128},... | collective-permute-start | bytes 27656 | tf_op jit(solution)/shard_map/ppermute | solution.py:15
  76.6 16.1 %collective-permute-start.14 = (f32[9,8,16,2]{2,1,3,0:T(8,128)}, f32[9,8,16,2]{2,1,3,0:T(8,128)}, u32[]{:S(2)}, u32[]{:S(2)}) collective-permute-start(f32[9,8,16,2]{2,1,3,0:T(8,128)} %copy.110), channel_id=1, source_target_pairs={{16,0},{32,16},{48,32},{64,48},{80,64},{96,80},{112,96},{128,112},... | collective-permute-start | bytes 27656 | tf_op jit(solution)/shard_map/ppermute | solution.py:17
  81.4 15.8 %collective-permute-start.15 = (f32[9,8,2,128]{3,1,2,0:T(8,128)}, f32[9,8,2,128]{3,1,2,0:T(8,128)}, u32[]{:S(2)}, u32[]{:S(2)}) collective-permute-start(f32[9,8,2,128]{3,1,2,0:T(8,128)} %copy.113), channel_id=1, source_target_pairs={{0,2},{2,4},{4,6},{6,8},{8,10},{10,12},{12,14},{1,3},{3,5},{5,7},{... | collective-permute-start | bytes 221192 | tf_op jit(solution)/shard_map/ppermute | solution.py:15
  84.0 14.2 %collective-permute-start.16 = (f32[9,8,2,128]{3,1,2,0:T(8,128)}, f32[9,8,2,128]{3,1,2,0:T(8,128)}, u32[]{:S(2)}, u32[]{:S(2)}) collective-permute-start(f32[9,8,2,128]{3,1,2,0:T(8,128)} %copy.114), channel_id=1, source_target_pairs={{2,0},{4,2},{6,4},{8,6},{10,8},{12,10},{14,12},{3,1},{5,3},{7,5},{... | collective-permute-start | bytes 221192 | tf_op jit(solution)/shard_map/ppermute | solution.py:17
  97.1 2.1 %copy-start.3 = (f32[8,19,128]{2,1,0:T(8,128)S(1)}, f32[8,19,128]{2,1,0:T(8,128)}, u32[]{:S(2)}) copy-start(f32[8,19,128]{2,1,0:T(8,128)} %get-tuple-element.56) | copy-start | bytes 233476
  97.2 2.1 %copy-start.6 = (f32[8,19,128]{2,1,0:T(8,128)S(1)}, f32[8,19,128]{2,1,0:T(8,128)}, u32[]{:S(2)}) copy-start(f32[8,19,128]{2,1,0:T(8,128)} %get-tuple-element.57) | copy-start | bytes 233476
  99.2 0.9 copy-start.10
  99.3 0.9 copy-start.12
  102.1 0.9 copy-start.15
  102.1 0.9 copy-start.14
  102.1 0.9 copy-start.13
  103.2 5.9 %collective-permute-start.17 = (f32[9,1,16,128]{3,2,1,0:T(8,128)S(1)}, f32[9,1,16,128]{3,2,1,0:T(8,128)S(1)}, u32[]{:S(2)}, u32[]{:S(2)}) collective-permute-start(f32[9,1,16,128]{3,2,1,0:T(8,128)S(1)} %get-tuple-element.40), channel_id=1, source_target_pairs={{0,1},{2,3},{4,5},{6,7},{8,9},{10,11},{12,13},{14,15},{16,17},{18,... | collective-permute-start | bytes 221192 | tf_op jit(solution)/shard_map/ppermute | solution.py:15
  104.5 4.6 %collective-permute-start.18 = (f32[9,1,16,128]{3,2,1,0:T(8,128)S(1)}, f32[9,1,16,128]{3,2,1,0:T(8,128)S(1)}, u32[]{:S(2)}, u32[]{:S(2)}) collective-permute-start(f32[9,1,16,128]{3,2,1,0:T(8,128)S(1)} %get-tuple-element.41), channel_id=1, source_target_pairs={{1,0},{3,2},{5,4},{7,6},{9,8},{11,10},{13,12},{15,14},{17,16},{19,... | collective-permute-start | bytes 221192 | tf_op jit(solution)/shard_map/ppermute | solution.py:17
  110.0 13.1 %collective-permute-start.19 = (f32[9,8,16,2]{2,1,3,0:T(8,128)S(1)}, f32[9,8,16,2]{2,1,3,0:T(8,128)S(1)}, u32[]{:S(2)}, u32[]{:S(2)}) collective-permute-start(f32[9,8,16,2]{2,1,3,0:T(8,128)S(1)} %copy.117), channel_id=1, source_target_pairs={{0,16},{16,32},{32,48},{48,64},{64,80},{80,96},{96,112},{112,128},... | collective-permute-start | bytes 27656 | tf_op jit(solution)/shard_map/ppermute | solution.py:15
  110.6 13.0 %collective-permute-start.20 = (f32[9,8,16,2]{2,1,3,0:T(8,128)S(1)}, f32[9,8,16,2]{2,1,3,0:T(8,128)}, u32[]{:S(2)}, u32[]{:S(2)}) collective-permute-start(f32[9,8,16,2]{2,1,3,0:T(8,128)S(1)} %copy.118), channel_id=1, source_target_pairs={{16,0},{32,16},{48,32},{64,48},{80,64},{96,80},{112,96},{128,112},... | collective-permute-start | bytes 27656 | tf_op jit(solution)/shard_map/ppermute | solution.py:17
  114.8 11.1 %collective-permute-start.21 = (f32[9,8,2,128]{3,1,2,0:T(8,128)S(1)}, f32[9,8,2,128]{3,1,2,0:T(8,128)S(1)}, u32[]{:S(2)}, u32[]{:S(2)}) collective-permute-start(f32[9,8,2,128]{3,1,2,0:T(8,128)S(1)} %copy.121), channel_id=1, source_target_pairs={{0,2},{2,4},{4,6},{6,8},{8,10},{10,12},{12,14},{1,3},{3,5},{5,7},{... | collective-permute-start | bytes 221192 | tf_op jit(solution)/shard_map/ppermute | solution.py:15
  116.8 9.3 %collective-permute-start.22 = (f32[9,8,2,128]{3,1,2,0:T(8,128)S(1)}, f32[9,8,2,128]{3,1,2,0:T(8,128)S(1)}, u32[]{:S(2)}, u32[]{:S(2)}) collective-permute-start(f32[9,8,2,128]{3,1,2,0:T(8,128)S(1)} %copy.122), channel_id=1, source_target_pairs={{2,0},{4,2},{6,4},{8,6},{10,8},{12,10},{14,12},{3,1},{5,3},{7,5},{... | collective-permute-start | bytes 221192 | tf_op jit(solution)/shard_map/ppermute | solution.py:17
  125.9 0.9 copy-start.4
  125.9 0.9 copy-start.7
